TPU v7x, 128 devices: a whole 4x4x4 slice. The times are simulated.
128 devices in a mesh: mat: 8 (over x, core), frac: 16 (over z, y).
Axes of the slice: x: 4, y: 4, z: 4, core: 2. Of those that a mesh axis runs over, the one named last changes fastest.
Arguments:
- pressure_start: float32 [128, 1024, 256], P('mat', 'frac'), may hold values from -6 to 6
- face_trans: float32 [3, 128, 1024, 256], P(None, 'mat', 'frac'), may hold values from 0.2 to 2
- cell_coef: float32 [128, 1024, 256], P('mat', 'frac'), may hold values from 0.05 to 0.5
- matrix_source: float32 [128, 1024, 256], P('mat', 'frac'), may hold values from -6 to 6
- mortar_owner: int32 [65536, 1], P(('mat', 'frac')), may hold values from 0 to 127; in each aligned block of 512 rows (0 to 511, 512 to 1023, ...) at most 8 rows name the same one
- mortar_cell: int32 [65536], P(('mat', 'frac')), may hold values from 0 to 262143
- mortar_frac: int32 [65536], P(('mat', 'frac')), may hold values from 0 to 16383
- mortar_kappa: float32 [65536], P(('mat', 'frac')), may hold values from 0.5 to 2
- tiles: float32 [128, 4, 128, 128], P('frac'), may hold values from -0.25 to 0.25
- tile_cols: int32 [128, 4], P('frac'), may hold values from 0 to 127
- frac_diag: float32 [16384], P('frac'), may hold values from 4 to 8
- frac_source: float32 [16384], P('frac'), may hold values from -6 to 6
- fracture_start: float32 [16384], P('frac'), may hold values from -6 to 6
Outputs:
- pressure: float32 [128, 1024, 256], P('mat', 'frac')
- fracture: float32 [16384], P('frac')
- flux: float32 [65536], P(('mat', 'frac'))
Inputs may be any that keep to these rules, and one draw needn't show every extreme that they name: `mortar_owner`: among the 512 mortar cells of one device, at most 8 name the same owner, and in some devices some owner is named exactly 8 times.
All inputs are finite; a program needn't handle non-finite values.
Results may differ from a plain program's by a relative error of at most 0.00015.
Values sent between devices are 32-bit elements; how exact they have to be, the bound alone decides.
No kernel may reach another device: no remote copies, remote signals or barrier semaphores. Data moves between devices by JAX's collectives and lax.ppermute only.
A program may use at most 128 MiB of HBM per device.

v0:
```python
import jax
import jax.numpy as jnp
from jax import lax
from jax.sharding import PartitionSpec as P

SWEEPS = 2
CG_ITERS = 3
OUTER = 2
relax_weight = 0.8


def with_halo(block, sides, width):
    for axis, dim in sides:
        count = lax.axis_size(axis)
        forward = [(i, i + 1) for i in range(count - 1)]
        backward = [(target, source) for source, target in forward]
        low = lax.ppermute(
            lax.slice_in_dim(block, block.shape[dim] - width, None, axis=dim), axis, forward
        )
        high = lax.ppermute(lax.slice_in_dim(block, 0, width, axis=dim), axis, backward)
        block = jnp.concatenate([low, block, high], axis=dim)
    return block


def copy_for_each(x, axis):
    length = lax.axis_size(axis)
    return lax.all_to_all(jnp.broadcast_to(x[None], (length, *x.shape)), axis, 0, 0, tiled=True)


def in_order(blocks, dim):
    lengths = list(blocks.shape[1:])
    lengths[dim] *= blocks.shape[0]
    return jnp.moveaxis(blocks, 0, dim).reshape(lengths)


def gather_directly(x, axis, dim):
    blocks = copy_for_each(x, axis)
    return in_order(blocks, dim)


def split_up(x, dim, length):
    lengths = x.shape
    blocks = x.reshape(*lengths[:dim], length, lengths[dim] // length, *lengths[dim + 1 :])
    return jnp.moveaxis(blocks, dim, 0)


def summed_on_arrival(x, axis, dim):
    length = lax.axis_size(axis)
    blocks = lax.all_to_all(split_up(x, dim, length), axis, 0, 0, tiled=True)
    return jnp.sum(blocks, axis=0)


def of_everyone(x, axis):
    return copy_for_each(x, axis).sum(axis=0)


def in_one(arrays, axis):
    ends = [0]
    for a in arrays:
        ends.append(ends[-1] + a.size)
    running = of_everyone(jnp.concatenate([a.ravel() for a in arrays]), axis)
    return tuple((running[b:e].reshape(a.shape) for a, b, e in zip(arrays, ends, ends[1:])))


def shift_next(values, along):
    padding = [(0, 0)] * values.ndim
    padding[along] = (0, 1)
    return lax.slice_in_dim(jnp.pad(values, padding), 1, values.shape[along] + 1, axis=along)


def shift_prev(values, along):
    padding = [(0, 0)] * values.ndim
    padding[along] = (1, 0)
    return lax.slice_in_dim(jnp.pad(values, padding), 0, values.shape[along], axis=along)


def relax(padded, coef_part, source_part, inside):
    centre = padded[1:-1, 1:-1]
    tx_here = coef_part[0, 1:-1, 1:-1]
    tx_low = coef_part[0, :-2, 1:-1]
    ty_here = coef_part[1, 1:-1, 1:-1]
    ty_low = coef_part[1, 1:-1, :-2]
    tz_here = coef_part[2, 1:-1, 1:-1]
    tz_low = shift_prev(tz_here, 2)
    cell_part = coef_part[3, 1:-1, 1:-1]
    base_part = coef_part[4, 1:-1, 1:-1]
    diagonal = cell_part + tx_here + tx_low + ty_here + ty_low + tz_here + tz_low
    diagonal = jnp.where(inside, diagonal, 1.0)
    applied = (
        diagonal * centre
        - tx_here * padded[2:, 1:-1]
        - tx_low * padded[:-2, 1:-1]
        - ty_here * padded[1:-1, 2:]
        - ty_low * padded[1:-1, :-2]
        - tz_here * shift_next(centre, 2)
        - tz_low * shift_prev(centre, 2)
    )
    updated = centre + relax_weight * (base_part + source_part - applied) / diagonal
    return jnp.where(inside, updated, 0.0)


def body(
    pressure_start,
    face_trans,
    cell_coef,
    matrix_source,
    mortar_owner,
    mortar_cell,
    mortar_frac,
    mortar_kappa,
    tiles,
    tile_cols,
    frac_diag,
    frac_source,
    fracture_start,
):
    width_x, width_y, depth_z = pressure_start.shape
    cells = width_x * width_y * depth_z
    mat_count = lax.axis_size("mat")
    frac_count = lax.axis_size("frac")
    devices = mat_count * frac_count
    row_mat = lax.axis_index("mat")
    row_frac = lax.axis_index("frac")
    size_b = tiles.shape[2]
    coefs = jnp.concatenate([face_trans, cell_coef[None], matrix_source[None]], 0)
    coef_ext = with_halo(coefs, (("mat", 1), ("frac", 2)), SWEEPS)
    owner = mortar_owner[:, 0]
    mortar_count = owner.shape[0]
    capacity = max(2, 2 * mortar_count // devices)
    rows = jnp.arange(mortar_count, dtype=jnp.int32)
    earlier = (owner[:, None] == owner[None, :]) & (rows[None, :] < rows[:, None])
    slot = jnp.sum(earlier.astype(jnp.int32), axis=1)
    place = owner * capacity + slot
    index_slots = (
        jnp.full((devices * capacity,), cells, jnp.int32)
        .at[place]
        .set(mortar_cell)
        .reshape(devices, capacity)
    )
    asked = lax.all_to_all(index_slots, ("mat", "frac"), split_axis=0, concat_axis=0, tiled=True)
    asked_safe = jnp.minimum(asked, cells - 1)

    def fracture_apply(vector):
        whole = gather_directly(vector, "frac", 0)
        blocks = whole.reshape(-1, size_b)
        forward = jnp.einsum(
            "rtij,rtj->ri", tiles, blocks[tile_cols], precision=lax.Precision.HIGHEST
        )
        backward = jnp.einsum(
            "rtij,ri->rtj", tiles, vector.reshape(-1, size_b), precision=lax.Precision.HIGHEST
        )
        spread = jnp.zeros_like(blocks).at[tile_cols.reshape(-1)].add(backward.reshape(-1, size_b))
        returned = summed_on_arrival(spread, "frac", 0)
        return frac_diag * vector + 0.5 * (forward + returned).reshape(-1)

    def two_products(residual, image):
        return in_one((jnp.sum(residual * residual), jnp.sum(residual * image)), "frac")

    def solve_fracture(fracture, target):
        residual = target - fracture_apply(fracture)
        image = fracture_apply(residual)
        norm_now, product = two_products(residual, image)
        alpha = norm_now / product
        direction, along_image = (residual, image)
        for step in range(CG_ITERS):
            fracture = fracture + alpha * direction
            residual = residual - alpha * along_image
            if step + 1 < CG_ITERS:
                image = fracture_apply(residual)
                norm_next, product = two_products(residual, image)
                ratio = norm_next / norm_now
                alpha = norm_next / (product - ratio * norm_next / alpha)
                direction = residual + ratio * direction
                along_image = image + ratio * along_image
                norm_now = norm_next
        return fracture

    pressure = pressure_start
    fracture = fracture_start
    flux = jnp.zeros(mortar_kappa.shape, jnp.float32)
    for outer_no in range(OUTER):
        local_values = pressure.reshape(-1)[asked_safe]
        returned = lax.all_to_all(
            local_values, ("mat", "frac"), split_axis=0, concat_axis=0, tiled=True
        )
        trace = returned.reshape(-1)[place]
        fracture_whole = lax.all_gather(fracture, "frac", axis=0, tiled=True)
        flux = mortar_kappa * (trace - fracture_whole[mortar_frac])
        landed = jax.ops.segment_sum(flux, mortar_frac, num_segments=fracture_whole.shape[0])
        rows_part = summed_on_arrival(landed, "frac", 0)
        load = lax.psum(rows_part, "mat")
        fracture = solve_fracture(fracture, frac_source + load)
        flux_slots = (
            jnp.zeros((devices * capacity,), jnp.float32)
            .at[place]
            .set(flux)
            .reshape(devices, capacity)
        )
        arrived = lax.all_to_all(
            flux_slots, ("mat", "frac"), split_axis=0, concat_axis=0, tiled=True
        )
        source = jax.ops.segment_sum(
            arrived.reshape(-1), asked_safe.reshape(-1), num_segments=cells
        ).reshape(pressure.shape)
        stacked = with_halo(jnp.stack([pressure, source]), (("mat", 1), ("frac", 2)), SWEEPS)
        current = stacked[0]
        source_ext = stacked[1]
        for sweep_no in range(SWEEPS):
            span_x = current.shape[0]
            span_y = current.shape[1]
            coef_part = coef_ext[:, sweep_no : sweep_no + span_x, sweep_no : sweep_no + span_y]
            source_part = source_ext[
                sweep_no + 1 : sweep_no + span_x - 1, sweep_no + 1 : sweep_no + span_y - 1
            ]
            offset = SWEEPS - sweep_no - 1
            global_x = row_mat * width_x - offset + jnp.arange(span_x - 2)
            global_y = row_frac * width_y - offset + jnp.arange(span_y - 2)
            keep_x = (global_x >= 0) & (global_x < width_x * mat_count)
            keep_y = (global_y >= 0) & (global_y < width_y * frac_count)
            current = relax(
                current, coef_part, source_part, (keep_x[:, None] & keep_y[None, :])[:, :, None]
            )
        pressure = current
    return (pressure, fracture, flux)


def solution(mesh):
    in_specs = (
        P("mat", "frac", None),
        P(None, "mat", "frac", None),
        P("mat", "frac", None),
        P("mat", "frac", None),
        P(("mat", "frac"), None),
        P(("mat", "frac")),
        P(("mat", "frac")),
        P(("mat", "frac")),
        P("frac", None, None, None),
        P("frac", None),
        P("frac"),
        P("frac"),
        P("frac"),
    )
    out_specs = (P("mat", "frac", None), P("frac"), P(("mat", "frac")))
    return jax.shard_map(body, mesh=mesh, in_specs=in_specs, out_specs=out_specs, check_vma=False)
```

profile of v0, /device:TPU:32, one launch (start us, length us, event | category | flops | bytes accessed | tf_op | source)
XLA Modules:
  0.0 576.3 jit_solution(12743596823609701940)
XLA Ops:
  5.8 10.2 %all-to-all-start = ((s32[128,1,8]{2,1,0:T(1,128)}), s32[128,1,8]{2,1,0:T(1,128)S(1)}, u32[]{:S(2)}, u32[]{:S(2)}) async-start(s32[128,1,8]{2,1,0:T(1,128)} %bitcast.4), calls=%async_computation | async-start | bytes 131072 | tf_op jit(solution)/shard_map/all_to_all | solution.py:140
  30.4 6.2 %gather_fusion = f32[1024]{0:T(1024)S(1)} fusion(f32[262144]{0:T(1024)S(1)} %bitcast.374, s32[1024]{0:T(1024)S(1)} %broadcast_clamp_fusion), kind=kCustom, calls=%fused_computation | custom fusion | bytes 12288 | tf_op jit(solution)/shard_map/gather | solution.py:182
  37.2 9.9 %all-to-all-start.1 = ((f32[128,1,8]{2,1,0:T(1,128)}), f32[128,1,8]{2,1,0:T(1,128)S(1)}, u32[]{:S(2)}, u32[]{:S(2)}) async-start(f32[128,1,8]{2,1,0:T(1,128)} %bitcast.6), calls=%async_computation.1 | async-start | bytes 131072 | tf_op jit(solution)/shard_map/all_to_all | solution.py:183
  47.1 24.0 %all_gather.6 = f32[16384]{0:T(1024)S(1)} all-gather(f32[1024]{0:T(1024)S(1)} %copy-done.25), channel_id=1, replica_groups=mesh['mat'=8,'frac'=16] {'frac'}, dimensions={0}, use_global_device_ids=true | all-gather | bytes 69632 | tf_op jit(solution)/shard_map/all_gather | solution.py:187
  81.3 7.6 %all-to-all-start.2 = ((f32[128,1,8]{2,1,0:T(1,128)}), f32[128,1,8]{2,1,0:T(1,128)S(1)}, u32[]{:S(2)}, u32[]{:S(2)}) async-start(f32[128,1,8]{2,1,0:T(1,128)} %bitcast.7), calls=%async_computation.2 | async-start | bytes 131072 | tf_op jit(solution)/shard_map/all_to_all | solution.py:199
  89.7 8.3 %all-to-all-done.2 = f32[128,1,8]{2,1,0:T(1,128)S(1)} async-done(((f32[128,1,8]{2,1,0:T(1,128)}), f32[128,1,8]{2,1,0:T(1,128)S(1)}, u32[]{:S(2)}, u32[]{:S(2)}) %all-to-all-start.2) | async-done | bytes 4128 | tf_op jit(solution)/shard_map/all_to_all | solution.py:199
  104.7 4.9 all-to-all-done.5
  109.6 4.8 all-to-all-start.6
  119.4 6.2 %scatter_custom_fusion.2 = f32[262144]{0:T(1024)S(1)} fusion(s32[1024]{0:T(1024)S(1)} %reshape.654, f32[1024]{0:T(1024)S(1)} %reshape.656, f32[]{:T(128)} %constant.26.clone.1), kind=kCustom, calls=%fused_computation.158 | custom fusion | flops 1024 | bytes 1048580 | tf_op jit(solution)/shard_map/scatter-add | solution.py:202
  127.5 7.3 %all-to-all-start.4 = ((f32[16,1,1024]{2,1,0:T(1,128)}), f32[16,1,1024]{2,1,0:T(1,128)S(1)}, u32[]{:S(2)}, u32[]{:S(2)}) async-start(f32[16,1,1024]{2,1,0:T(1,128)} %bitcast.26), calls=%async_computation.4 | async-start | bytes 131072 | tf_op jit(solution)/shard_map/all_to_all | solution.py:49
  141.0 12.4 %psum.14 = f32[1024]{0:T(1024)S(1)} all-reduce(f32[1024]{0:T(1024)S(1)} %reduce_sum.265), channel_id=1, replica_groups=mesh['mat'=8,'frac'=16] {'mat'}, use_global_device_ids=true, to_apply=%region_6.0 | all-reduce | flops 1024 | bytes 8192 | tf_op jit(solution)/shard_map/psum | solution.py:191
  154.2 4.8 all-to-all-start.7
  192.6 4.9 all-to-all-start.10
  234.0 5.2 all-to-all-start.13
  245.5 4.8 all-to-all-start.14
  275.4 4.9 all-to-all-start.18
  289.2 5.4 collective-permute-done.2
  312.1 5.9 %fusion.32 = (f32[18,66,256]{2,1,0:T(8,128)S(1)}, f32[18,66,256]{2,1,0:T(8,128)}) fusion(f32[18,66,256]{2,1,0:T(8,128)S(1)} %slice.369, f32[18,66,256]{2,1,0:T(8,128)S(1)} %slice_bitcast_fusion.4, f32[20,68,256]{2,1,0:T(8,128)S(1)} %get-tuple-element.29, f32[5,20,68,256]{3,2,1,0:T(8,128)S(1)} %pad_maximum_fusion, f32[20,68,256]{2,1,0:T(8,128)S(1)} %get-tuple-element.28, ...), kind=kLoop, calls=%fused_computation.95 | loop fusion | flops 9427968 | bytes 23790756 | tf_op jit(solution)/shard_map/jit(_where)/select_n | solution.py:99
  325.3 6.2 %gather_fusion.3 = f32[1024]{0:T(1024)S(1)} fusion(f32[262144]{0:T(1024)S(1)} %bitcast.375, s32[1024]{0:T(1024)S(1)} %broadcast_clamp_fusion), kind=kCustom, calls=%fused_computation.3 | custom fusion | bytes 12288 | tf_op jit(solution)/shard_map/gather | solution.py:182
  336.7 24.4 %all_gather.7 = f32[16384]{0:T(1024)S(1)} all-gather(f32[1024]{0:T(1024)S(1)} %multiply_add_fusion.1), channel_id=1, replica_groups=mesh['mat'=8,'frac'=16] {'frac'}, dimensions={0}, use_global_device_ids=true | all-gather | bytes 69632 | tf_op jit(solution)/shard_map/all_gather | solution.py:187
  366.3 5.4 all-to-all-start.19
  378.3 9.4 %all-to-all-start.16 = ((f32[128,1,8]{2,1,0:T(1,128)}), f32[128,1,8]{2,1,0:T(1,128)S(1)}, u32[]{:S(2)}, u32[]{:S(2)}) async-start(f32[128,1,8]{2,1,0:T(1,128)} %bitcast.96), calls=%async_computation.16 | async-start | bytes 131072 | tf_op jit(solution)/shard_map/all_to_all | solution.py:199
  402.3 7.2 %scatter_custom_fusion.9 = f32[262144]{0:T(1024)} fusion(s32[1024]{0:T(1024)} %copy-done.47, f32[1024]{0:T(1024)S(1)} %reshape.712, f32[]{:T(128)} %constant.26.clone.1), kind=kCustom, calls=%fused_computation.156 | custom fusion | flops 1024 | bytes 1049088 | tf_op jit(solution)/shard_map/scatter-add | solution.py:202
  414.0 14.1 %psum.15 = f32[1024]{0:T(1024)S(1)} all-reduce(f32[1024]{0:T(1024)S(1)} %reduce_sum.279), channel_id=1, replica_groups=mesh['mat'=8,'frac'=16] {'mat'}, use_global_device_ids=true, to_apply=%region_28.29 | all-reduce | flops 1024 | bytes 8192 | tf_op jit(solution)/shard_map/psum | solution.py:191
  428.7 7.2 %all-to-all-start.20 = ((f32[16,1,1024]{2,1,0:T(1,128)}), f32[16,1,1024]{2,1,0:T(1,128)S(1)}, u32[]{:S(2)}, u32[]{:S(2)}) async-start(f32[16,1,1024]{2,1,0:T(1,128)} %broadcast_in_dim.112), calls=%async_computation.20 | async-start | bytes 131072 | tf_op jit(solution)/shard_map/all_to_all | solution.py:27
  442.2 4.8 all-to-all-start.21
  469.3 5.1 all-to-all-start.23
  480.7 4.8 all-to-all-start.24
  510.9 4.9 all-to-all-start.26
  522.1 4.8 all-to-all-start.27
  535.3 10.7 %all_to_all.187 = f32[16,1,2]{2,1,0:T(1,128)S(1)} all-to-all(f32[16,1,2]{2,1,0:T(1,128)S(1)} %broadcast_in_dim.217), channel_id=1, replica_groups=mesh['mat'=8,'frac'=16] {'frac'}, dimensions={0} | all-to-all | bytes 256 | tf_op jit(solution)/shard_map/all_to_all | solution.py:27
  558.2 5.9 %collective-permute-done.10 = f32[2,20,2,256]{3,2,1,0:T(2,128)S(1)} collective-permute-done((f32[2,20,2,256]{3,2,1,0:T(2,128)S(1)}, f32[2,20,2,256]{3,2,1,0:T(2,128)S(1)}, u32[]{:S(2)}, u32[]{:S(2)}) %collective-permute-start.10) | collective-permute-done | bytes 81952 | tf_op jit(solution)/shard_map/ppermute | solution.py:17
  (325 shorter events, 302.7 us)
Async XLA Ops:
  5.8 24.3 %all-to-all-start = ((s32[128,1,8]{2,1,0:T(1,128)}), s32[128,1,8]{2,1,0:T(1,128)S(1)}, u32[]{:S(2)}, u32[]{:S(2)}) async-start(s32[128,1,8]{2,1,0:T(1,128)} %bitcast.4), calls=%async_computation | async-start | bytes 131072 | tf_op jit(solution)/shard_map/all_to_all | solution.py:140
  18.6 277.3 %collective-permute-start.5 = (f32[5,2,64,256]{3,2,1,0:T(8,128)}, f32[5,2,64,256]{3,2,1,0:T(8,128)}, u32[]{:S(2)}, u32[]{:S(2)}) collective-permute-start(f32[5,2,64,256]{3,2,1,0:T(8,128)} %get-tuple-element.25), channel_id=1, source_target_pairs={{16,0},{32,16},{48,32},{64,48},{80,64},{96,80},{112,96},{17,1},{33... | collective-permute-start | bytes 1966088 | tf_op jit(solution)/shard_map/ppermute | solution.py:20
  20.0 275.9 %collective-permute-start.4 = (f32[5,2,64,256]{3,2,1,0:T(8,128)}, f32[5,2,64,256]{3,2,1,0:T(8,128)}, u32[]{:S(2)}, u32[]{:S(2)}) collective-permute-start(f32[5,2,64,256]{3,2,1,0:T(8,128)} %get-tuple-element.24), channel_id=1, source_target_pairs={{0,16},{16,32},{32,48},{48,64},{64,80},{80,96},{96,112},{1,17},{17... | collective-permute-start | bytes 1966088 | tf_op jit(solution)/shard_map/ppermute | solution.py:17
  37.2 37.0 %all-to-all-start.1 = ((f32[128,1,8]{2,1,0:T(1,128)}), f32[128,1,8]{2,1,0:T(1,128)S(1)}, u32[]{:S(2)}, u32[]{:S(2)}) async-start(f32[128,1,8]{2,1,0:T(1,128)} %bitcast.6), calls=%async_computation.1 | async-start | bytes 131072 | tf_op jit(solution)/shard_map/all_to_all | solution.py:183
  81.3 16.7 %all-to-all-start.2 = ((f32[128,1,8]{2,1,0:T(1,128)}), f32[128,1,8]{2,1,0:T(1,128)S(1)}, u32[]{:S(2)}, u32[]{:S(2)}) async-start(f32[128,1,8]{2,1,0:T(1,128)} %bitcast.7), calls=%async_computation.2 | async-start | bytes 131072 | tf_op jit(solution)/shard_map/all_to_all | solution.py:199
  98.7 10.8 %all-to-all-start.5 = ((f32[16,1,1024]{2,1,0:T(1,128)}), f32[16,1,1024]{2,1,0:T(1,128)S(1)}, u32[]{:S(2)}, u32[]{:S(2)}) async-start(f32[16,1,1024]{2,1,0:T(1,128)} %broadcast_in_dim.103), calls=%async_computation.5 | async-start | bytes 131072 | tf_op jit(solution)/shard_map/all_to_all | solution.py:27
  109.6 17.9 %all-to-all-start.6 = ((f32[16,8,128]{2,1,0:T(8,128)}), f32[16,8,128]{2,1,0:T(8,128)S(1)}, u32[]{:S(2)}, u32[]{:S(2)}) async-start(f32[16,8,128]{2,1,0:T(8,128)} %bitcast.40), calls=%async_computation.6 | async-start | bytes 131072 | tf_op jit(solution)/shard_map/all_to_all | solution.py:49
  127.5 13.5 %all-to-all-start.4 = ((f32[16,1,1024]{2,1,0:T(1,128)}), f32[16,1,1024]{2,1,0:T(1,128)S(1)}, u32[]{:S(2)}, u32[]{:S(2)}) async-start(f32[16,1,1024]{2,1,0:T(1,128)} %bitcast.26), calls=%async_computation.4 | async-start | bytes 131072 | tf_op jit(solution)/shard_map/all_to_all | solution.py:49
  154.2 11.1 %all-to-all-start.7 = ((f32[16,1,1024]{2,1,0:T(1,128)}), f32[16,1,1024]{2,1,0:T(1,128)S(1)}, u32[]{:S(2)}, u32[]{:S(2)}) async-start(f32[16,1,1024]{2,1,0:T(1,128)} %broadcast_in_dim.105), calls=%async_computation.7 | async-start | bytes 131072 | tf_op jit(solution)/shard_map/all_to_all | solution.py:27
  165.3 11.1 %all-to-all-start.8 = ((f32[16,8,128]{2,1,0:T(8,128)}), f32[16,8,128]{2,1,0:T(8,128)S(1)}, u32[]{:S(2)}, u32[]{:S(2)}) async-start(f32[16,8,128]{2,1,0:T(8,128)} %bitcast.55), calls=%async_computation.8 | async-start | bytes 131072 | tf_op jit(solution)/shard_map/all_to_all | solution.py:49
  179.1 10.8 %all-to-all-start.9 = ((f32[16,1,2]{2,1,0:T(1,128)}), f32[16,1,2]{2,1,0:T(1,128)S(1)}, u32[]{:S(2)}, u32[]{:S(2)}) async-start(f32[16,1,2]{2,1,0:T(1,128)} %broadcast_in_dim.106), calls=%async_computation.9 | async-start | bytes 16384 | tf_op jit(solution)/shard_map/all_to_all | solution.py:27
  192.6 11.2 %all-to-all-start.10 = ((f32[16,1,1024]{2,1,0:T(1,128)}), f32[16,1,1024]{2,1,0:T(1,128)S(1)}, u32[]{:S(2)}, u32[]{:S(2)}) async-start(f32[16,1,1024]{2,1,0:T(1,128)} %broadcast_in_dim.107), calls=%async_computation.10 | async-start | bytes 131072 | tf_op jit(solution)/shard_map/all_to_all | solution.py:27
  203.8 11.1 %all-to-all-start.11 = ((f32[16,8,128]{2,1,0:T(8,128)}), f32[16,8,128]{2,1,0:T(8,128)S(1)}, u32[]{:S(2)}, u32[]{:S(2)}) async-start(f32[16,8,128]{2,1,0:T(8,128)} %bitcast.73), calls=%async_computation.11 | async-start | bytes 131072 | tf_op jit(solution)/shard_map/all_to_all | solution.py:49
  222.2 58.1 %collective-permute-start.1 = (f32[2,2,64,256]{3,2,1,0:T(8,128)}, f32[2,2,64,256]{3,2,1,0:T(8,128)S(1)}, u32[]{:S(2)}, u32[]{:S(2)}) collective-permute-start(f32[2,2,64,256]{3,2,1,0:T(8,128)} %get-tuple-element.37), channel_id=1, source_target_pairs={{16,0},{32,16},{48,32},{64,48},{80,64},{96,80},{112,96},{17,1},{33... | collective-permute-start | bytes 786440 | tf_op jit(solution)/shard_map/ppermute | solution.py:20
  234.0 11.4 %all-to-all-start.13 = ((f32[16,1,1024]{2,1,0:T(1,128)}), f32[16,1,1024]{2,1,0:T(1,128)S(1)}, u32[]{:S(2)}, u32[]{:S(2)}) async-start(f32[16,1,1024]{2,1,0:T(1,128)} %broadcast_in_dim.109), calls=%async_computation.13 | async-start | bytes 131072 | tf_op jit(solution)/shard_map/all_to_all | solution.py:27
  245.5 11.1 %all-to-all-start.14 = ((f32[16,8,128]{2,1,0:T(8,128)}), f32[16,8,128]{2,1,0:T(8,128)S(1)}, u32[]{:S(2)}, u32[]{:S(2)}) async-start(f32[16,8,128]{2,1,0:T(8,128)} %bitcast.91), calls=%async_computation.14 | async-start | bytes 131072 | tf_op jit(solution)/shard_map/all_to_all | solution.py:49
  264.0 16.3 %collective-permute-start = (f32[2,2,64,256]{3,2,1,0:T(8,128)}, f32[2,2,64,256]{3,2,1,0:T(8,128)}, u32[]{:S(2)}, u32[]{:S(2)}) collective-permute-start(f32[2,2,64,256]{3,2,1,0:T(8,128)} %get-tuple-element.36), channel_id=1, source_target_pairs={{0,16},{16,32},{32,48},{48,64},{64,80},{80,96},{96,112},{1,17},{17... | collective-permute-start | bytes 786440 | tf_op jit(solution)/shard_map/ppermute | solution.py:17
  275.4 56.8 %all-to-all-start.18 = ((f32[16,1,1024]{2,1,0:T(1,128)}), f32[16,1,1024]{2,1,0:T(1,128)S(1)}, u32[]{:S(2)}, u32[]{:S(2)}) async-start(f32[16,1,1024]{2,1,0:T(1,128)} %broadcast_in_dim.111), calls=%async_computation.18 | async-start | bytes 131072 | tf_op jit(solution)/shard_map/all_to_all | solution.py:27
  332.2 34.1 %all-to-all-start.3 = ((f32[128,1,8]{2,1,0:T(1,128)}), f32[128,1,8]{2,1,0:T(1,128)S(1)}, u32[]{:S(2)}, u32[]{:S(2)}) async-start(f32[128,1,8]{2,1,0:T(1,128)} %bitcast.25), calls=%async_computation.3 | async-start | bytes 131072 | tf_op jit(solution)/shard_map/all_to_all | solution.py:183
  366.3 12.0 %all-to-all-start.19 = ((f32[16,8,128]{2,1,0:T(8,128)}), f32[16,8,128]{2,1,0:T(8,128)S(1)}, u32[]{:S(2)}, u32[]{:S(2)}) async-start(f32[16,8,128]{2,1,0:T(8,128)} %bitcast.112), calls=%async_computation.19 | async-start | bytes 131072 | tf_op jit(solution)/shard_map/all_to_all | solution.py:49
  378.3 18.6 %all-to-all-start.16 = ((f32[128,1,8]{2,1,0:T(1,128)}), f32[128,1,8]{2,1,0:T(1,128)S(1)}, u32[]{:S(2)}, u32[]{:S(2)}) async-start(f32[128,1,8]{2,1,0:T(1,128)} %bitcast.96), calls=%async_computation.16 | async-start | bytes 131072 | tf_op jit(solution)/shard_map/all_to_all | solution.py:199
  396.9 17.1 %all-to-all-start.17 = ((f32[16,1,1024]{2,1,0:T(1,128)}), f32[16,1,1024]{2,1,0:T(1,128)S(1)}, u32[]{:S(2)}, u32[]{:S(2)}) async-start(f32[16,1,1024]{2,1,0:T(1,128)} %bitcast.99), calls=%async_computation.17 | async-start | bytes 131072 | tf_op jit(solution)/shard_map/all_to_all | solution.py:49
  428.7 13.5 %all-to-all-start.20 = ((f32[16,1,1024]{2,1,0:T(1,128)}), f32[16,1,1024]{2,1,0:T(1,128)S(1)}, u32[]{:S(2)}, u32[]{:S(2)}) async-start(f32[16,1,1024]{2,1,0:T(1,128)} %broadcast_in_dim.112), calls=%async_computation.20 | async-start | bytes 131072 | tf_op jit(solution)/shard_map/all_to_all | solution.py:27
  442.2 11.1 %all-to-all-start.21 = ((f32[16,8,128]{2,1,0:T(8,128)}), f32[16,8,128]{2,1,0:T(8,128)S(1)}, u32[]{:S(2)}, u32[]{:S(2)}) async-start(f32[16,8,128]{2,1,0:T(8,128)} %bitcast.127), calls=%async_computation.21 | async-start | bytes 131072 | tf_op jit(solution)/shard_map/all_to_all | solution.py:49
  455.9 10.8 %all-to-all-start.22 = ((f32[16,1,2]{2,1,0:T(1,128)}), f32[16,1,2]{2,1,0:T(1,128)S(1)}, u32[]{:S(2)}, u32[]{:S(2)}) async-start(f32[16,1,2]{2,1,0:T(1,128)} %broadcast_in_dim.113), calls=%async_computation.22 | async-start | bytes 16384 | tf_op jit(solution)/shard_map/all_to_all | solution.py:27
  460.7 89.8 %collective-permute-start.9 = (f32[2,2,64,256]{3,2,1,0:T(8,128)}, f32[2,2,64,256]{3,2,1,0:T(8,128)S(1)}, u32[]{:S(2)}, u32[]{:S(2)}) collective-permute-start(f32[2,2,64,256]{3,2,1,0:T(8,128)} %get-tuple-element.35), channel_id=1, source_target_pairs={{16,0},{32,16},{48,32},{64,48},{80,64},{96,80},{112,96},{17,1},{33... | collective-permute-start | bytes 786440 | tf_op jit(solution)/shard_map/ppermute | solution.py:20
  469.3 11.4 %all-to-all-start.23 = ((f32[16,1,1024]{2,1,0:T(1,128)}), f32[16,1,1024]{2,1,0:T(1,128)S(1)}, u32[]{:S(2)}, u32[]{:S(2)}) async-start(f32[16,1,1024]{2,1,0:T(1,128)} %broadcast_in_dim.114), calls=%async_computation.23 | async-start | bytes 131072 | tf_op jit(solution)/shard_map/all_to_all | solution.py:27
  480.7 11.1 %all-to-all-start.24 = ((f32[16,8,128]{2,1,0:T(8,128)}), f32[16,8,128]{2,1,0:T(8,128)S(1)}, u32[]{:S(2)}, u32[]{:S(2)}) async-start(f32[16,8,128]{2,1,0:T(8,128)} %bitcast.145), calls=%async_computation.24 | async-start | bytes 131072 | tf_op jit(solution)/shard_map/all_to_all | solution.py:49
  494.4 10.8 %all-to-all-start.25 = ((f32[16,1,2]{2,1,0:T(1,128)}), f32[16,1,2]{2,1,0:T(1,128)S(1)}, u32[]{:S(2)}, u32[]{:S(2)}) async-start(f32[16,1,2]{2,1,0:T(1,128)} %broadcast_in_dim.115), calls=%async_computation.25 | async-start | bytes 16384 | tf_op jit(solution)/shard_map/all_to_all | solution.py:27
  499.2 51.4 %collective-permute-start.8 = (f32[2,2,64,256]{3,2,1,0:T(8,128)}, f32[2,2,64,256]{3,2,1,0:T(8,128)}, u32[]{:S(2)}, u32[]{:S(2)}) collective-permute-start(f32[2,2,64,256]{3,2,1,0:T(8,128)} %get-tuple-element.34), channel_id=1, source_target_pairs={{0,16},{16,32},{32,48},{48,64},{64,80},{80,96},{96,112},{1,17},{17... | collective-permute-start | bytes 786440 | tf_op jit(solution)/shard_map/ppermute | solution.py:17
  510.9 11.2 %all-to-all-start.26 = ((f32[16,1,1024]{2,1,0:T(1,128)}), f32[16,1,1024]{2,1,0:T(1,128)S(1)}, u32[]{:S(2)}, u32[]{:S(2)}) async-start(f32[16,1,1024]{2,1,0:T(1,128)} %broadcast_in_dim.216), calls=%async_computation.26 | async-start | bytes 131072 | tf_op jit(solution)/shard_map/all_to_all | solution.py:27
  522.1 11.1 %all-to-all-start.27 = ((f32[16,8,128]{2,1,0:T(8,128)}), f32[16,8,128]{2,1,0:T(8,128)S(1)}, u32[]{:S(2)}, u32[]{:S(2)}) async-start(f32[16,8,128]{2,1,0:T(8,128)} %bitcast.163), calls=%async_computation.27 | async-start | bytes 131072 | tf_op jit(solution)/shard_map/all_to_all | solution.py:49
  (61 other events, 1090.6 us)
where the time goes:
time: 587 us; the launch traced here: 576 us
  starting transfers between devices  188 us (32%)
  waiting for transfers between devices  103 us (18%)
  blocking collectives  85.6 us (15%)
  other arithmetic  83.5 us (14%)
  local copies, waits for them, and re-layouts  69.9 us (12%)
  matrix products  25.7 us (4%)
  between operations  21.3 us (4%)
    all_to_all x13, starting transfers between devices, copy_for_each(): lax.all_to_all(jnp.broadcast_to(x[None], (length, *x.shape)), axis, 0, 0,...  65.3 us
    all_to_all x10, starting transfers between devices, summed_on_arrival(): blocks = lax.all_to_all(split_up(x, dim, length), axis, 0, 0, tiled=True)  50.7 us
    all_to_all x13, waiting for transfers between devices, copy_for_each(): lax.all_to_all(jnp.broadcast_to(x[None], (length, *x.shape)), axis, 0, 0,...  49.9 us
    all_gather x2, blocking collectives, body(): fracture_whole = lax.all_gather(fracture, 'frac', axis=0, tiled=True)  48.4 us
    psum x2, blocking collectives, body(): load = lax.psum(rows_part, 'mat')  26.5 us
    all_to_all x10, waiting for transfers between devices, summed_on_arrival(): blocks = lax.all_to_all(split_up(x, dim, length), axis, 0, 0, tiled=True)  24 us
    all_to_all x2, starting transfers between devices, body(): lax.all_to_all(flux_slots, ('mat', 'frac'), split_axis=0, concat_axis=0,...  16.9 us
    dot_general x8, matrix products, fracture_apply(): jnp.einsum('rtij,rtj->ri', tiles, blocks[tile_cols], precision=lax.Precis...  16.8 us
  transfers between devices with their start and end apart: 40, of which 25 were waited for; matrix products, arithmetic and copies ran while one was open for 26% of the time, Pallas kernels for 0%

commit v1 on v0

--- a/solution.py
+++ b/solution.py
@@ -2,6 +2,7 @@
 import jax.numpy as jnp
 from jax import lax
 from jax.sharding import PartitionSpec as P
+from jax.lax import axis_index, axis_size, ppermute
 
 SWEEPS = 2
 CG_ITERS = 3
@@ -184,7 +185,38 @@
             local_values, ("mat", "frac"), split_axis=0, concat_axis=0, tiled=True
         )
         trace = returned.reshape(-1)[place]
-        fracture_whole = lax.all_gather(fracture, "frac", axis=0, tiled=True)
+        local_now = axis_size("frac")
+        mixed_arr = axis_index("frac")
+        res, val2, outer = (local_now, mixed_arr, fracture.shape[0])
+        seen = []
+        for p, hop_no in enumerate(fracture.shape):
+            seen.append(hop_no * res if p == 0 else hop_no)
+        fracture_whole = lax.dynamic_update_slice_in_dim(
+            jnp.zeros(seen, fracture.dtype), fracture, val2 * outer, axis=0
+        )
+        latest = fresh = fracture
+        ix = 1
+        while ix < res // 2 + 1:
+            windows = []
+            p = 0
+            while p < res:
+                windows.append((p, (p + 1) % res))
+                p += 1
+            latest = ppermute(latest, "frac", windows)
+            fracture_whole = lax.dynamic_update_slice_in_dim(
+                fracture_whole, latest, (val2 - ix) % res * outer, axis=0
+            )
+            if 2 * ix < res:
+                pool = []
+                p = 0
+                while p < res:
+                    pool.append((p, (p - 1) % res))
+                    p += 1
+                fresh = ppermute(fresh, "frac", pool)
+                fracture_whole = lax.dynamic_update_slice_in_dim(
+                    fracture_whole, fresh, (val2 + ix) % res * outer, axis=0
+                )
+            ix += 1
         flux = mortar_kappa * (trace - fracture_whole[mortar_frac])
         landed = jax.ops.segment_sum(flux, mortar_frac, num_segments=fracture_whole.shape[0])
         rows_part = summed_on_arrival(landed, "frac", 0)

time: 587 us -> 632 us (1.077)
  the two profiles are of different devices: /device:TPU:32 before, /device:TPU:24 now
where the time goes in v1:
time: 632 us; the launch traced here: 620 us
  starting transfers between devices  262 us (41%)
  waiting for transfers between devices  88.2 us (14%)
  other arithmetic  83.6 us (13%)
  local copies, waits for them, and re-layouts  80.3 us (13%)
  blocking collectives  58.7 us (9%)
  matrix products  24.9 us (4%)
  between operations  22.3 us (4%)
    all_to_all x11, starting transfers between devices, copy_for_each(): lax.all_to_all(jnp.broadcast_to(x[None], (length, *x.shape)), axis, 0, 0,...  66.1 us
    all_to_all x10, starting transfers between devices, summed_on_arrival(): blocks = lax.all_to_all(split_up(x, dim, length), axis, 0, 0, tiled=True)  61.7 us
    ppermute x16, starting transfers between devices, body(): latest = ppermute(latest, 'frac', windows)  50.5 us
    all_to_all x11, waiting for transfers between devices, copy_for_each(): lax.all_to_all(jnp.broadcast_to(x[None], (length, *x.shape)), axis, 0, 0,...  33.8 us
    all_to_all x3, blocking collectives, copy_for_each(): lax.all_to_all(jnp.broadcast_to(x[None], (length, *x.shape)), axis, 0, 0,...  32.2 us
    psum x2, blocking collectives, body(): load = lax.psum(rows_part, 'mat')  26.5 us
    all_to_all x10, waiting for transfers between devices, summed_on_arrival(): blocks = lax.all_to_all(split_up(x, dim, length), axis, 0, 0, tiled=True)  22.5 us
    all_to_all x2, starting transfers between devices, body(): lax.all_to_all(local_values, ('mat', 'frac'), split_axis=0, concat_axis=0...  21.1 us
  transfers between devices with their start and end apart: 68, of which 29 were waited for; matrix products, arithmetic and copies ran while one was open for 27% of the time, Pallas kernels for 0%

profile of v1, /device:TPU:24, one launch (start us, length us, event | category | flops | bytes accessed | tf_op | source)
XLA Modules:
  0.0 619.9 jit_solution(16179446036425798801)
XLA Ops:
  7.8 10.3 %all-to-all-start = ((s32[128,1,8]{2,1,0:T(1,128)}), s32[128,1,8]{2,1,0:T(1,128)S(1)}, u32[]{:S(2)}, u32[]{:S(2)}) async-start(s32[128,1,8]{2,1,0:T(1,128)} %bitcast.4), calls=%async_computation | async-start | bytes 131072 | tf_op jit(solution)/shard_map/all_to_all | solution.py:141
  36.8 6.1 gather_fusion
  43.7 8.4 %all-to-all-start.1 = ((f32[128,1,8]{2,1,0:T(1,128)}), f32[128,1,8]{2,1,0:T(1,128)S(1)}, u32[]{:S(2)}, u32[]{:S(2)}) async-start(f32[128,1,8]{2,1,0:T(1,128)} %bitcast.6), calls=%async_computation.1 | async-start | bytes 131072 | tf_op jit(solution)/shard_map/all_to_all | solution.py:184
  62.6 9.8 %all-to-all-start.5 = ((f32[16,1,1024]{2,1,0:T(1,128)}), f32[16,1,1024]{2,1,0:T(1,128)S(1)}, u32[]{:S(2)}, u32[]{:S(2)}) async-start(f32[16,1,1024]{2,1,0:T(1,128)} %broadcast_in_dim.103), calls=%async_computation.5 | async-start | bytes 131072 | tf_op jit(solution)/shard_map/all_to_all | solution.py:28
  101.3 10.3 %all-to-all-start.6 = ((f32[16,8,128]{2,1,0:T(8,128)}), f32[16,8,128]{2,1,0:T(8,128)S(1)}, u32[]{:S(2)}, u32[]{:S(2)}) async-start(f32[16,8,128]{2,1,0:T(8,128)} %bitcast.40), calls=%async_computation.6 | async-start | bytes 131072 | tf_op jit(solution)/shard_map/all_to_all | solution.py:50
  117.3 6.0 all-to-all-start.4
  129.0 12.4 %psum.14 = f32[1024]{0:T(1024)S(1)} all-reduce(f32[1024]{0:T(1024)S(1)} %reduce_sum.265), channel_id=1, replica_groups=mesh['mat'=8,'frac'=16] {'mat'}, use_global_device_ids=true, to_apply=%region_6.7 | all-reduce | flops 1024 | bytes 8192 | tf_op jit(solution)/shard_map/psum | solution.py:223
  142.1 5.4 all-to-all-start.7
  153.3 5.4 all-to-all-start.8
  166.4 10.7 %all_to_all.187 = f32[16,1,2]{2,1,0:T(1,128)S(1)} all-to-all(f32[16,1,2]{2,1,0:T(1,128)S(1)} %broadcast_in_dim.106), channel_id=1, replica_groups=mesh['mat'=8,'frac'=16] {'frac'}, dimensions={0} | all-to-all | bytes 256 | tf_op jit(solution)/shard_map/all_to_all | solution.py:28
  179.7 5.5 all-to-all-start.10
  191.0 5.4 all-to-all-start.11
  204.2 10.7 %all_to_all.188 = f32[16,1,2]{2,1,0:T(1,128)S(1)} all-to-all(f32[16,1,2]{2,1,0:T(1,128)S(1)} %broadcast_in_dim.108), channel_id=1, replica_groups=mesh['mat'=8,'frac'=16] {'frac'}, dimensions={0} | all-to-all | bytes 256 | tf_op jit(solution)/shard_map/all_to_all | solution.py:28
  232.1 5.4 all-to-all-start.14
  251.2 5.6 all-to-all-done.15
  266.8 6.5 %all-to-all-start.2 = ((f32[128,1,8]{2,1,0:T(1,128)}), f32[128,1,8]{2,1,0:T(1,128)S(1)}, u32[]{:S(2)}, u32[]{:S(2)}) async-start(f32[128,1,8]{2,1,0:T(1,128)} %bitcast.7), calls=%async_computation.2 | async-start | bytes 131072 | tf_op jit(solution)/shard_map/all_to_all | solution.py:231
  282.5 6.9 %scatter_custom_fusion.2 = f32[262144]{0:T(1024)} fusion(s32[1024]{0:T(1024)S(1)} %reshape.654, f32[1024]{0:T(1024)S(1)} %reshape.656, f32[]{:T(128)} %constant.163.clone.1), kind=kCustom, calls=%fused_computation.158 | custom fusion | flops 1024 | bytes 1048580 | tf_op jit(solution)/shard_map/scatter-add | solution.py:234
  307.3 5.7 collective-permute-done.30
  320.1 6.0 collective-permute-start.17
  333.7 6.0 all-to-all-start.18
  361.8 5.9 fusion.32
  375.1 6.2 gather_fusion.3
  382.1 12.8 %all-to-all-start.3 = ((f32[128,1,8]{2,1,0:T(1,128)}), f32[128,1,8]{2,1,0:T(1,128)S(1)}, u32[]{:S(2)}, u32[]{:S(2)}) async-start(f32[128,1,8]{2,1,0:T(1,128)} %bitcast.25), calls=%async_computation.3 | async-start | bytes 131072 | tf_op jit(solution)/shard_map/all_to_all | solution.py:184
  407.6 7.7 %all-to-all-start.19 = ((f32[16,8,128]{2,1,0:T(8,128)}), f32[16,8,128]{2,1,0:T(8,128)S(1)}, u32[]{:S(2)}, u32[]{:S(2)}) async-start(f32[16,8,128]{2,1,0:T(8,128)} %bitcast.112), calls=%async_computation.19 | async-start | bytes 131072 | tf_op jit(solution)/shard_map/all_to_all | solution.py:50
  421.9 9.3 %all-to-all-start.16 = ((f32[128,1,8]{2,1,0:T(1,128)}), f32[128,1,8]{2,1,0:T(1,128)S(1)}, u32[]{:S(2)}, u32[]{:S(2)}) async-start(f32[128,1,8]{2,1,0:T(1,128)} %bitcast.96), calls=%async_computation.16 | async-start | bytes 131072 | tf_op jit(solution)/shard_map/all_to_all | solution.py:231
  439.5 5.4 all-to-all-start.17
  445.9 7.4 %scatter_custom_fusion.9 = f32[262144]{0:T(1024)} fusion(s32[1024]{0:T(1024)} %copy-done.44, f32[1024]{0:T(1024)S(1)} %reshape.712, f32[]{:T(128)} %constant.163.clone.1), kind=kCustom, calls=%fused_computation.156 | custom fusion | flops 1024 | bytes 1049088 | tf_op jit(solution)/shard_map/scatter-add | solution.py:234
  457.7 14.1 %psum.15 = f32[1024]{0:T(1024)S(1)} all-reduce(f32[1024]{0:T(1024)S(1)} %reduce_sum.279), channel_id=1, replica_groups=mesh['mat'=8,'frac'=16] {'mat'}, use_global_device_ids=true, to_apply=%region_28.29 | all-reduce | flops 1024 | bytes 8192 | tf_op jit(solution)/shard_map/psum | solution.py:223
  472.5 7.2 %all-to-all-start.20 = ((f32[16,1,1024]{2,1,0:T(1,128)}), f32[16,1,1024]{2,1,0:T(1,128)S(1)}, u32[]{:S(2)}, u32[]{:S(2)}) async-start(f32[16,1,1024]{2,1,0:T(1,128)} %broadcast_in_dim.112), calls=%async_computation.20 | async-start | bytes 131072 | tf_op jit(solution)/shard_map/all_to_all | solution.py:28
  524.0 5.4 all-to-all-start.24
  578.9 10.7 %all_to_all.189 = f32[16,1,2]{2,1,0:T(1,128)S(1)} all-to-all(f32[16,1,2]{2,1,0:T(1,128)S(1)} %broadcast_in_dim.217), channel_id=1, replica_groups=mesh['mat'=8,'frac'=16] {'frac'}, dimensions={0} | all-to-all | bytes 256 | tf_op jit(solution)/shard_map/all_to_all | solution.py:28
  602.1 5.7 collective-permute-done.41
  (452 shorter events, 351.4 us)
Async XLA Ops:
  0.6 28.8 %collective-permute-start = (f32[1024]{0:T(1024)}, f32[1024]{0:T(1024)S(1)}, u32[]{:S(2)}, u32[]{:S(2)}) collective-permute-start(f32[1024]{0:T(1024)} %param.25), channel_id=1, source_target_pairs={{0,1},{1,2},{2,3},{3,4},{4,5},{5,6},{6,7},{7,8},{8,9},{9,10},{10,1... | collective-permute-start | bytes 12296 | tf_op jit(solution)/shard_map/ppermute | solution.py:205
  2.3 28.9 %collective-permute-start.1 = (f32[1024]{0:T(1024)}, f32[1024]{0:T(1024)S(1)}, u32[]{:S(2)}, u32[]{:S(2)}) collective-permute-start(f32[1024]{0:T(1024)} %param.25), channel_id=1, source_target_pairs={{0,15},{1,0},{2,1},{3,2},{4,3},{5,4},{6,5},{7,6},{8,7},{9,8},{10,9... | collective-permute-start | bytes 12296 | tf_op jit(solution)/shard_map/ppermute | solution.py:215
  7.8 21.5 %all-to-all-start = ((s32[128,1,8]{2,1,0:T(1,128)}), s32[128,1,8]{2,1,0:T(1,128)S(1)}, u32[]{:S(2)}, u32[]{:S(2)}) async-start(s32[128,1,8]{2,1,0:T(1,128)} %bitcast.4), calls=%async_computation | async-start | bytes 131072 | tf_op jit(solution)/shard_map/all_to_all | solution.py:141
  20.6 325.0 %collective-permute-start.19 = (f32[5,2,64,256]{3,2,1,0:T(8,128)}, f32[5,2,64,256]{3,2,1,0:T(8,128)}, u32[]{:S(2)}, u32[]{:S(2)}) collective-permute-start(f32[5,2,64,256]{3,2,1,0:T(8,128)} %get-tuple-element.26), channel_id=1, source_target_pairs={{0,16},{16,32},{32,48},{48,64},{64,80},{80,96},{96,112},{1,17},{17... | collective-permute-start | bytes 1966088 | tf_op jit(solution)/shard_map/ppermute | solution.py:18
  31.2 20.8 %collective-permute-start.3 = (f32[1024]{0:T(1024)S(1)}, f32[1024]{0:T(1024)S(1)}, u32[]{:S(2)}, u32[]{:S(2)}) collective-permute-start(f32[1024]{0:T(1024)S(1)} %collective-permute-done.1), channel_id=1, source_target_pairs={{0,15},{1,0},{2,1},{3,2},{4,3},{5,4},{6,5},{7,6},{8,7},{9,8},{10,9... | collective-permute-start | bytes 12296 | tf_op jit(solution)/shard_map/ppermute | solution.py:215
  33.1 19.8 %collective-permute-start.4 = (f32[1024]{0:T(1024)S(1)}, f32[1024]{0:T(1024)S(1)}, u32[]{:S(2)}, u32[]{:S(2)}) collective-permute-start(f32[1024]{0:T(1024)S(1)} %collective-permute-done.2), channel_id=1, source_target_pairs={{0,1},{1,2},{2,3},{3,4},{4,5},{5,6},{6,7},{7,8},{8,9},{9,10},{10,1... | collective-permute-start | bytes 12296 | tf_op jit(solution)/shard_map/ppermute | solution.py:205
  43.7 18.3 %all-to-all-start.1 = ((f32[128,1,8]{2,1,0:T(1,128)}), f32[128,1,8]{2,1,0:T(1,128)S(1)}, u32[]{:S(2)}, u32[]{:S(2)}) async-start(f32[128,1,8]{2,1,0:T(1,128)} %bitcast.6), calls=%async_computation.1 | async-start | bytes 131072 | tf_op jit(solution)/shard_map/all_to_all | solution.py:184
  57.8 14.7 %collective-permute-start.7 = (f32[1024]{0:T(1024)S(1)}, f32[1024]{0:T(1024)S(1)}, u32[]{:S(2)}, u32[]{:S(2)}) collective-permute-start(f32[1024]{0:T(1024)S(1)} %collective-permute-done.5), channel_id=1, source_target_pairs={{0,15},{1,0},{2,1},{3,2},{4,3},{5,4},{6,5},{7,6},{8,7},{9,8},{10,9... | collective-permute-start | bytes 12296 | tf_op jit(solution)/shard_map/ppermute | solution.py:215
  57.8 15.7 %collective-permute-start.8 = (f32[1024]{0:T(1024)S(1)}, f32[1024]{0:T(1024)S(1)}, u32[]{:S(2)}, u32[]{:S(2)}) collective-permute-start(f32[1024]{0:T(1024)S(1)} %collective-permute-done.6), channel_id=1, source_target_pairs={{0,1},{1,2},{2,3},{3,4},{4,5},{5,6},{6,7},{7,8},{8,9},{9,10},{10,1... | collective-permute-start | bytes 12296 | tf_op jit(solution)/shard_map/ppermute | solution.py:205
  62.6 38.7 %all-to-all-start.5 = ((f32[16,1,1024]{2,1,0:T(1,128)}), f32[16,1,1024]{2,1,0:T(1,128)S(1)}, u32[]{:S(2)}, u32[]{:S(2)}) async-start(f32[16,1,1024]{2,1,0:T(1,128)} %broadcast_in_dim.103), calls=%async_computation.5 | async-start | bytes 131072 | tf_op jit(solution)/shard_map/all_to_all | solution.py:28
  84.1 13.5 %collective-permute-start.13 = (f32[1024]{0:T(1024)S(1)}, f32[1024]{0:T(1024)S(1)}, u32[]{:S(2)}, u32[]{:S(2)}) collective-permute-start(f32[1024]{0:T(1024)S(1)} %collective-permute-done.11), channel_id=1, source_target_pairs={{0,15},{1,0},{2,1},{3,2},{4,3},{5,4},{6,5},{7,6},{8,7},{9,8},{10,9... | collective-permute-start | bytes 12296 | tf_op jit(solution)/shard_map/ppermute | solution.py:215
  84.1 13.8 %collective-permute-start.14 = (f32[1024]{0:T(1024)S(1)}, f32[1024]{0:T(1024)S(1)}, u32[]{:S(2)}, u32[]{:S(2)}) collective-permute-start(f32[1024]{0:T(1024)S(1)} %collective-permute-done.12), channel_id=1, source_target_pairs={{0,1},{1,2},{2,3},{3,4},{4,5},{5,6},{6,7},{7,8},{8,9},{9,10},{10,1... | collective-permute-start | bytes 12296 | tf_op jit(solution)/shard_map/ppermute | solution.py:205
  101.3 16.0 %all-to-all-start.6 = ((f32[16,8,128]{2,1,0:T(8,128)}), f32[16,8,128]{2,1,0:T(8,128)S(1)}, u32[]{:S(2)}, u32[]{:S(2)}) async-start(f32[16,8,128]{2,1,0:T(8,128)} %bitcast.40), calls=%async_computation.6 | async-start | bytes 131072 | tf_op jit(solution)/shard_map/all_to_all | solution.py:50
  261.5 12.7 %collective-permute-start.23 = (f32[1024]{0:T(1024)S(1)}, f32[1024]{0:T(1024)S(1)}, u32[]{:S(2)}, u32[]{:S(2)}) collective-permute-start(f32[1024]{0:T(1024)S(1)} %get-tuple-element.17), channel_id=1, source_target_pairs={{0,1},{1,2},{2,3},{3,4},{4,5},{5,6},{6,7},{7,8},{8,9},{9,10},{10,1... | collective-permute-start | bytes 12296 | tf_op jit(solution)/shard_map/ppermute | solution.py:205
  266.8 14.7 %all-to-all-start.2 = ((f32[128,1,8]{2,1,0:T(1,128)}), f32[128,1,8]{2,1,0:T(1,128)S(1)}, u32[]{:S(2)}, u32[]{:S(2)}) async-start(f32[128,1,8]{2,1,0:T(1,128)} %bitcast.7), calls=%async_computation.2 | async-start | bytes 131072 | tf_op jit(solution)/shard_map/all_to_all | solution.py:231
  273.3 18.7 %collective-permute-start.24 = (f32[1024]{0:T(1024)S(1)}, f32[1024]{0:T(1024)S(1)}, u32[]{:S(2)}, u32[]{:S(2)}) collective-permute-start(f32[1024]{0:T(1024)S(1)} %get-tuple-element.17), channel_id=1, source_target_pairs={{0,15},{1,0},{2,1},{3,2},{4,3},{5,4},{6,5},{7,6},{8,7},{9,8},{10,9... | collective-permute-start | bytes 12296 | tf_op jit(solution)/shard_map/ppermute | solution.py:215
  274.2 18.5 %collective-permute-start.25 = (f32[1024]{0:T(1024)S(1)}, f32[1024]{0:T(1024)S(1)}, u32[]{:S(2)}, u32[]{:S(2)}) collective-permute-start(f32[1024]{0:T(1024)S(1)} %collective-permute-done.23), channel_id=1, source_target_pairs={{0,1},{1,2},{2,3},{3,4},{4,5},{5,6},{6,7},{7,8},{8,9},{9,10},{10,1... | collective-permute-start | bytes 12296 | tf_op jit(solution)/shard_map/ppermute | solution.py:205
  297.4 16.2 %collective-permute-start.15 = (f32[2,2,64,256]{3,2,1,0:T(8,128)S(1)}, f32[2,2,64,256]{3,2,1,0:T(8,128)S(1)}, u32[]{:S(2)}, u32[]{:S(2)}) collective-permute-start(f32[2,2,64,256]{3,2,1,0:T(8,128)S(1)} %get-tuple-element.38), channel_id=1, source_target_pairs={{0,16},{16,32},{32,48},{48,64},{64,80},{80,96},{96,112},{1,17},{17... | collective-permute-start | bytes 786440 | tf_op jit(solution)/shard_map/ppermute | solution.py:18
  298.7 20.6 %collective-permute-start.16 = (f32[2,2,64,256]{3,2,1,0:T(8,128)S(1)}, f32[2,2,64,256]{3,2,1,0:T(8,128)S(1)}, u32[]{:S(2)}, u32[]{:S(2)}) collective-permute-start(f32[2,2,64,256]{3,2,1,0:T(8,128)S(1)} %get-tuple-element.39), channel_id=1, source_target_pairs={{16,0},{32,16},{48,32},{64,48},{80,64},{96,80},{112,96},{17,1},{33... | collective-permute-start | bytes 786440 | tf_op jit(solution)/shard_map/ppermute | solution.py:21
  305.8 39.8 %collective-permute-start.20 = (f32[5,2,64,256]{3,2,1,0:T(8,128)}, f32[5,2,64,256]{3,2,1,0:T(8,128)}, u32[]{:S(2)}, u32[]{:S(2)}) collective-permute-start(f32[5,2,64,256]{3,2,1,0:T(8,128)} %get-tuple-element.27), channel_id=1, source_target_pairs={{16,0},{32,16},{48,32},{64,48},{80,64},{96,80},{112,96},{17,1},{33... | collective-permute-start | bytes 1966088 | tf_op jit(solution)/shard_map/ppermute | solution.py:21
  320.1 20.6 %collective-permute-start.17 = (f32[2,20,2,256]{3,2,1,0:T(2,128)}, f32[2,20,2,256]{3,2,1,0:T(2,128)}, u32[]{:S(2)}, u32[]{:S(2)}) collective-permute-start(f32[2,20,2,256]{3,2,1,0:T(2,128)} %get-tuple-element.34), channel_id=1, source_target_pairs={{0,1},{1,2},{2,3},{3,4},{4,5},{5,6},{6,7},{7,8},{8,9},{9,10},{10,1... | collective-permute-start | bytes 245768 | tf_op jit(solution)/shard_map/ppermute | solution.py:18
  326.2 17.8 %collective-permute-start.18 = (f32[2,20,2,256]{3,2,1,0:T(2,128)}, f32[2,20,2,256]{3,2,1,0:T(2,128)}, u32[]{:S(2)}, u32[]{:S(2)}) collective-permute-start(f32[2,20,2,256]{3,2,1,0:T(2,128)} %get-tuple-element.35), channel_id=1, source_target_pairs={{1,0},{2,1},{3,2},{4,3},{5,4},{6,5},{7,6},{8,7},{9,8},{10,9},{11,1... | collective-permute-start | bytes 245768 | tf_op jit(solution)/shard_map/ppermute | solution.py:21
  333.7 48.4 %all-to-all-start.18 = ((f32[16,1,1024]{2,1,0:T(1,128)}), f32[16,1,1024]{2,1,0:T(1,128)S(1)}, u32[]{:S(2)}, u32[]{:S(2)}) async-start(f32[16,1,1024]{2,1,0:T(1,128)} %broadcast_in_dim.111), calls=%async_computation.18 | async-start | bytes 131072 | tf_op jit(solution)/shard_map/all_to_all | solution.py:28
  339.8 62.4 %collective-permute-start.36 = (f32[1024]{0:T(1024)}, f32[1024]{0:T(1024)}, u32[]{:S(2)}, u32[]{:S(2)}) collective-permute-start(f32[1024]{0:T(1024)} %copy-done.65), channel_id=1, source_target_pairs={{0,15},{1,0},{2,1},{3,2},{4,3},{5,4},{6,5},{7,6},{8,7},{9,8},{10,9... | collective-permute-start | bytes 12296 | tf_op jit(solution)/shard_map/ppermute | solution.py:215
  340.7 62.3 %collective-permute-start.37 = (f32[1024]{0:T(1024)}, f32[1024]{0:T(1024)}, u32[]{:S(2)}, u32[]{:S(2)}) collective-permute-start(f32[1024]{0:T(1024)} %collective-permute-done.35), channel_id=1, source_target_pairs={{0,1},{1,2},{2,3},{3,4},{4,5},{5,6},{6,7},{7,8},{8,9},{9,10},{10,1... | collective-permute-start | bytes 12296 | tf_op jit(solution)/shard_map/ppermute | solution.py:205
  382.1 25.5 %all-to-all-start.3 = ((f32[128,1,8]{2,1,0:T(1,128)}), f32[128,1,8]{2,1,0:T(1,128)S(1)}, u32[]{:S(2)}, u32[]{:S(2)}) async-start(f32[128,1,8]{2,1,0:T(1,128)} %bitcast.25), calls=%async_computation.3 | async-start | bytes 131072 | tf_op jit(solution)/shard_map/all_to_all | solution.py:184
  407.6 14.3 %all-to-all-start.19 = ((f32[16,8,128]{2,1,0:T(8,128)}), f32[16,8,128]{2,1,0:T(8,128)S(1)}, u32[]{:S(2)}, u32[]{:S(2)}) async-start(f32[16,8,128]{2,1,0:T(8,128)} %bitcast.112), calls=%async_computation.19 | async-start | bytes 131072 | tf_op jit(solution)/shard_map/all_to_all | solution.py:50
  421.9 17.6 %all-to-all-start.16 = ((f32[128,1,8]{2,1,0:T(1,128)}), f32[128,1,8]{2,1,0:T(1,128)S(1)}, u32[]{:S(2)}, u32[]{:S(2)}) async-start(f32[128,1,8]{2,1,0:T(1,128)} %bitcast.96), calls=%async_computation.16 | async-start | bytes 131072 | tf_op jit(solution)/shard_map/all_to_all | solution.py:231
  439.5 18.2 %all-to-all-start.17 = ((f32[16,1,1024]{2,1,0:T(1,128)}), f32[16,1,1024]{2,1,0:T(1,128)S(1)}, u32[]{:S(2)}, u32[]{:S(2)}) async-start(f32[16,1,1024]{2,1,0:T(1,128)} %bitcast.99), calls=%async_computation.17 | async-start | bytes 131072 | tf_op jit(solution)/shard_map/all_to_all | solution.py:50
  472.5 12.9 %all-to-all-start.20 = ((f32[16,1,1024]{2,1,0:T(1,128)}), f32[16,1,1024]{2,1,0:T(1,128)S(1)}, u32[]{:S(2)}, u32[]{:S(2)}) async-start(f32[16,1,1024]{2,1,0:T(1,128)} %broadcast_in_dim.112), calls=%async_computation.20 | async-start | bytes 131072 | tf_op jit(solution)/shard_map/all_to_all | solution.py:28
  504.6 89.6 %collective-permute-start.38 = (f32[2,2,64,256]{3,2,1,0:T(8,128)}, f32[2,2,64,256]{3,2,1,0:T(8,128)S(1)}, u32[]{:S(2)}, u32[]{:S(2)}) collective-permute-start(f32[2,2,64,256]{3,2,1,0:T(8,128)} %get-tuple-element.36), channel_id=1, source_target_pairs={{0,16},{16,32},{32,48},{48,64},{64,80},{80,96},{96,112},{1,17},{17... | collective-permute-start | bytes 786440 | tf_op jit(solution)/shard_map/ppermute | solution.py:18
  543.1 51.0 %collective-permute-start.39 = (f32[2,2,64,256]{3,2,1,0:T(8,128)}, f32[2,2,64,256]{3,2,1,0:T(8,128)}, u32[]{:S(2)}, u32[]{:S(2)}) collective-permute-start(f32[2,2,64,256]{3,2,1,0:T(8,128)} %get-tuple-element.37), channel_id=1, source_target_pairs={{16,0},{32,16},{48,32},{64,48},{80,64},{96,80},{112,96},{17,1},{33... | collective-permute-start | bytes 786440 | tf_op jit(solution)/shard_map/ppermute | solution.py:21
  (108 other events, 1934.6 us)
